TPU v7x, 256 devices: a whole 4x4x8 slice. The times are simulated.
256 devices in a mesh: mom: 4 (over x_hi, core), en: 64 (over y, z, x_lo).
Axes of the slice: x: 4 (x_hi: 2, x_lo: 2; x = x_hi * 2 + x_lo), y: 4, z: 8, core: 2. Of those that a mesh axis runs over, the one named last changes fastest.
Arguments:
- green_less: bfloat16 [8, 1536, 8, 288], P('mom', 'en'), may hold values from -6 to 6
- green_greater: bfloat16 [8, 1536, 8, 288], P('mom', 'en'), may hold values from -6 to 6
- derivative: float32 [2, 3, 144], replicated, may hold values from -1.75 to 1.75
- neighbours: int32 [2, 4], replicated, may hold values from 0 to 1
- phonon: bfloat16 [2, 8, 24, 3, 8], replicated, may hold values from 0.0099487305 to 0.099609375
Outputs:
- self_energy: bfloat16 [8, 1536, 8, 288], P('mom', 'en')
- polarisation: float32 [8, 24, 3, 8], P('mom')
All inputs are finite; a program needn't handle non-finite values.
Results may differ from a plain program's by a relative error of at most 0.0034.
Values may be sent and summed in bfloat16 or wider, within the bound.
A program may use at most 64 MiB of HBM per device.

v0:
```python
import functools

import jax
import jax.numpy as jnp
import numpy as np
from jax import lax
from jax.experimental import pallas as pl
from jax.experimental.pallas import tpu as pltpu
from jax.sharding import PartitionSpec as P

NO = 12
NB = 4
NN = NO * NO
MAIN = 256
TAIL = 2 * NN - MAIN
WIDE = MAIN + 128
NX = 2
MESH = pl.DeviceIdType.MESH
BF = jnp.bfloat16
F32 = jnp.float32
NT = (((1,), (1,)), ((), ()))


def tables():
    r = np.arange(NN)
    col = np.arange(2 * NN)
    sub = col % NN
    rows_s = (r[None, :] % NO == r[:, None] // NO).astype(np.float32)
    rows_t = (r[None, :] % NO == r[:, None] % NO).astype(np.float32)
    cols_i = np.zeros((NN, WIDE), np.float32)
    cols_u = np.zeros((NN, WIDE), np.float32)
    cols_i[:, : 2 * NN] = r[:, None] // NO == sub[None, :] // NO
    cols_u[:, : 2 * NN] = r[:, None] // NO == sub[None, :] % NO
    swap = np.zeros((WIDE, WIDE), np.float32)
    flipped = (col // NN) * NN + (sub % NO) * NO + sub // NO
    swap[flipped, col] = np.where(col < NN, 1.0, -1.0)
    return rows_s, rows_t, cols_i, cols_u, swap


def split(x):
    hi = x.astype(BF)
    return hi, (x - hi.astype(F32)).astype(BF)


def kernel(
    dims,
    gl_hbm, gg_hbm, der_hbm, nb_hbm, ph_hbm, rs_hbm, rt_hbm, ci_hbm, cu_hbm, swap_hbm,
    se_ref, pol_ref,
    gl_in, gg_in, der_ref, nb_ref, ph_ref, rs_ref, rt_ref, ci_ref, cu_ref, swap_ref,
    rows_f, gl_t, gg_t, gl_r, gg_r, gl, gl_tail, gg_tail, coef, toe, kr_hi, kr_lo, wgt, acc,
    se_t, se_r, part, got_z, plane, got_p,
    loads, s_gg, r_gg, s_own, s_halo, r_gl, s_se, r_se, s_z, r_z, s_p, r_p,
):
    moms, ens, ny, nz, own_k, own_e, pairs, momenta, window_n = dims
    rows = own_k * own_e
    all_rows = momenta * own_e
    span = 32 * momenta
    groups = rows // 8
    me = lax.axis_index("mom")
    en = lax.axis_index("en")
    ring, ix = en // NX, en % NX
    iy, iz = ring // nz, ring % nz
    rings = ens // NX
    above_ring, below_ring = lax.rem(ring + 1, rings), lax.rem(ring + rings - 1, rings)
    pair = me * NX + ix

    hbm = (gg_hbm, gl_hbm, ph_hbm, der_hbm, nb_hbm, rs_hbm, rt_hbm, ci_hbm, cu_hbm, swap_hbm)
    near = (gg_in, gl_in, ph_ref, der_ref, nb_ref, rs_ref, rt_ref, ci_ref, cu_ref, swap_ref)
    fetch = [pltpu.make_async_copy(a, b, loads.at[i]) for i, (a, b) in enumerate(zip(hbm, near))]
    for copy in fetch:
        copy.start()

    barrier = pltpu.get_barrier_semaphore()

    def greet(mom_at, en_at):
        pl.semaphore_signal(
            barrier, inc=1, device_id={"mom": mom_at, "en": en_at}, device_id_type=MESH
        )

    mom_of = [me] + [lax.rem(me + rel, moms) for rel in range(1, moms)]
    ix_of = [ix, 1 - ix]
    mates = [(rx, rm) for rx in range(NX) for rm in range(moms)]
    for rx, rm in mates:
        if rx or rm:
            greet(mom_of[rm], ring * NX + ix_of[rx])
        greet(mom_of[rm], above_ring * NX + ix_of[rx])
        greet(mom_of[rm], below_ring * NX + ix_of[rx])
    z_of = [(iy * nz + lax.rem(iz + rel, nz)) * NX + ix for rel in range(nz)]
    for rel in range(1, nz):
        greet(me, z_of[rel])
    y_of = [lax.rem(iy + ry, ny) for ry in range(ny)]
    flats = [(ry, rx, rm) for ry in range(ny) for rx in range(NX) for rm in range(moms)][1:]
    for ry, rx, rm in flats:
        if ry:
            greet(mom_of[rm], (y_of[ry] * nz + iz) * NX + ix_of[rx])
    greeted = 3 * len(mates) - 1 + nz - 1 + (ny - 1) * len(mates)

    lane8 = lax.broadcasted_iota(jnp.int32, (8, 128), 1)

    def pack_tail(x):
        halves = [jnp.zeros((8, 128), F32), jnp.zeros((8, 128), F32)]
        for g in range(groups):
            y = x[8 * g : 8 * (g + 1)]
            at = TAIL * (g % 4)
            y = pltpu.roll(y, at, 1) if at else y
            keep = (lane8 >= at) & (lane8 < at + TAIL)
            halves[g // 4] = jnp.where(keep, y, halves[g // 4])
        return jnp.concatenate(halves, axis=1)

    def unpack_tail(x):
        found = []
        for g in range(groups):
            y = x[:, 128 * (g // 4) : 128 * (g // 4 + 1)]
            at = TAIL * (g % 4)
            y = pltpu.roll(y, 128 - at, 1) if at else y
            found.append(jnp.where(lane8 < TAIL, y, 0.0))
        return found

    def by_pair(src, dst):
        whole = src[...].astype(F32).reshape(rows * pairs, 2 * NN)
        rows_f[0] = whole[:, :128]
        rows_f[1] = whole[:, 128:MAIN]
        rows_f[2, :, :TAIL] = whole[:, MAIN:]
        for p in range(pairs):
            x = [rows_f.at[c][pl.ds(p, rows, stride=pairs), :] for c in range(3)]
            dst[p, :rows, :128] = x[0].astype(BF)
            dst[p, :rows, 128:] = x[1].astype(BF)
            dst[p, rows:, :] = pack_tail(x[2]).astype(BF)

    def remote(src, dst, send, recv, mom_at, en_at):
        return pltpu.make_async_remote_copy(
            src_ref=src, dst_ref=dst, send_sem=send, recv_sem=recv,
            device_id={"mom": mom_at, "en": en_at}, device_id_type=MESH,
        )

    def landed(ref, sem):
        pltpu.make_async_copy(ref, ref, sem).wait()

    sent = []

    def send(copy):
        copy.start()
        sent.append(copy)

    fetch[0].wait()
    by_pair(gg_in, gg_t)
    pl.semaphore_wait(barrier, greeted)
    for i, (rx, rm) in enumerate(mates):
        if i:
            to = mom_of[rm] * NX + ix_of[rx]
            send(remote(
                gg_t.at[to], gg_r.at[ix, me], s_gg.at[i], r_gg.at[ix, me],
                mom_of[rm], ring * NX + ix_of[rx],
            ))
    fetch[1].wait()
    by_pair(gl_in, gl_t)
    for i, (rx, rm) in enumerate(mates):
        if i:
            to = mom_of[rm] * NX + ix_of[rx]
            send(remote(
                gl_t.at[to], gl_r.at[1 + ix, me], s_own.at[i], r_gl.at[1 + ix, me],
                mom_of[rm], ring * NX + ix_of[rx],
            ))
    slot = 3 - 3 * ix
    other_ring = lax.rem(ring + rings + 2 * ix - 1, rings)
    for i, (rx, rm) in enumerate(mates):
        to = mom_of[rm] * NX + ix_of[rx]
        send(remote(
            gl_t.at[to], gl_r.at[slot, me], s_halo.at[i], r_gl.at[slot, me],
            mom_of[rm], other_ring * NX + ix_of[rx],
        ))
    gg_r[ix, me] = gg_t[pair]
    gl_r[1 + ix, me] = gl_t[pair]

    def await_ring(buffer, first, sems):
        for i, (rx, rm) in enumerate(mates):
            if i:
                at = first + ix_of[rx]
                landed(buffer.at[at, mom_of[rm]], sems.at[at, mom_of[rm]])

    gl[:, :, own_e:, :] = jnp.zeros((4, momenta, 32 - own_e, MAIN), BF)
    gl_tail[:, :, own_e:, :] = jnp.zeros((4, momenta, 32 - own_e, 128), BF)

    for copy in fetch[2:]:
        copy.wait()

    first_part = lax.broadcasted_iota(jnp.int32, (NN, WIDE), 1) < NN

    def expand(row, rows_of, cols_of):
        hi, lo = split(row)
        out = jnp.dot(rows_of * hi, cols_of, preferred_element_type=F32)
        return out + jnp.dot(rows_of * lo, cols_of, preferred_element_type=F32)

    def block_of(m, index):
        found = der_ref[m, 0:1, :]
        for i in range(1, der_ref.shape[1]):
            found = jnp.where(index == i, der_ref[m, i : i + 1, :], found)
        return found

    cut = MAIN - NN
    other = nb_ref[pair // NB, lax.rem(pair, NB)]
    for m in range(3):
        left = expand(block_of(m, pair // NB), rs_ref[...], ci_ref[...])
        right = expand(block_of(m, other), rt_ref[...], cu_ref[...])
        both = left * right
        top = jnp.where(first_part, both, 0.0)
        low = jnp.where(first_part, 0.0, both)
        for dst, a, b in zip((kr_hi, kr_lo), split(top), split(low)):
            dst[m, :NN, :] = a
            dst[m, NN : 2 * NN, :] = b
            dst[m, 2 * NN :, :] = jnp.zeros((WIDE - 2 * NN, WIDE), BF)

    lane = lax.broadcasted_iota(jnp.int32, (own_e, 128), 1)
    row = lax.broadcasted_iota(jnp.int32, (own_e, 128), 0)
    spot = lax.rem(lane, 32)

    def turn(lo, hi, n):
        n = n % span
        if n >= 128:
            lo, hi, n = hi, lo, n - 128
        if n == 0:
            return lo, hi
        a, b = pltpu.roll(lo, n, 1), pltpu.roll(hi, n, 1)
        keep = lane >= n
        return jnp.where(keep, a, b), jnp.where(keep, b, a)

    def slide(at, index):
        lo, hi = (coef.at[at, side][pl.ds(index, own_e, stride=0), :] for side in range(2))
        a = pltpu.roll(lo, 0, 1, stride=1, stride_axis=0)
        b = pltpu.roll(hi, 0, 1, stride=1, stride_axis=0)
        keep = lane >= row
        return jnp.where(keep, a, b), jnp.where(keep, b, a)

    lines = 3 * pairs
    w_at = lax.broadcasted_iota(jnp.int32, (window_n, 128), 0)
    l_at = lax.broadcasted_iota(jnp.int32, (window_n, 128), 1)
    places = (l_at == window_n - 1 - w_at, l_at == w_at)
    for s in range(2):
        flat = ph_ref[s].reshape(momenta * lines, window_n)
        spread = jnp.dot(
            flat, jnp.where(places[s], 1.0, 0.0).astype(BF), preferred_element_type=F32
        )
        sides = [None, None]
        for q in range(momenta):
            block = (momenta - q) % momenta
            x = spread[lines * q : lines * (q + 1)]
            if block % 4:
                x = pltpu.roll(x, 32 * (block % 4), 1)
            sides[block // 4] = x if sides[block // 4] is None else sides[block // 4] + x
        for at, n in ((2 * s, (0, 1)[s]), (2 * s + 1, (span - window_n, span + 1 - window_n)[s])):
            lo, hi = turn(sides[0], sides[1], n)
            coef[at, 0] = lo
            coef[at, 1] = hi

    for m in range(3):
        index = m * pairs + pair
        absorb, absorb_own = slide(0, index), slide(1, index)
        emit_own, emit = slide(2, index), slide(3, index)
        for step in range(3):
            pick = []
            for side in range(2):
                if step == 0:
                    x = jnp.where(spot >= row, absorb[side], 0.0)
                elif step == 1:
                    x = jnp.where(spot >= row, emit_own[side], absorb_own[side])
                else:
                    x = jnp.where(spot <= row, emit[side], 0.0)
                pick.append(x)
            for k in range(0, momenta, 2):
                even, odd = turn(*pick, 32 * k), turn(*pick, 32 * (k + 1))
                at = m * all_rows + k * own_e
                for side in range(2):
                    both = jnp.concatenate([even[side], odd[side]], axis=0)
                    toe[step, at : at + 2 * own_e, 128 * side : 128 * (side + 1)] = both.astype(BF)

    has_low = (ring > 0).astype(F32)
    has_up = (ring < rings - 1).astype(F32)

    await_ring(gg_r, 0, r_gg)
    for i in range(NX):
        for a in range(moms):
            tails = unpack_tail(gg_r[i, a, rows:, :].astype(F32))
            gg_tail[i, rows * a : rows * (a + 1), :] = jnp.concatenate(tails, axis=0).astype(BF)
        block = jnp.concatenate(
            [gg_r[i, :, :rows, :].reshape(all_rows, MAIN), gg_tail[i]], axis=1
        )
        swapped = jnp.dot(block, swap_ref[...], preferred_element_type=F32).astype(BF)
        for m in range(3):
            w = lax.dot_general(swapped, kr_hi[m], NT, preferred_element_type=F32)
            w = w + lax.dot_general(swapped, kr_lo[m], NT, preferred_element_type=F32)
            wgt[i, m] = w.astype(BF)

    def spread_rows(j):
        for a in range(moms):
            for k in range(own_k):
                gl[j, own_k * a + k, :own_e, :] = gl_r[j, a, own_e * k : own_e * (k + 1), :]
            tails = unpack_tail(gl_r[j, a, rows:, :].astype(F32))
            for k in range(own_k):
                x = jnp.concatenate(tails[3 * k : 3 * (k + 1)], axis=0)
                gl_tail[j, own_k * a + k, :own_e, :] = x.astype(BF)

    def block_at(j):
        return jnp.concatenate(
            [gl[j].reshape(span, MAIN), gl_tail[j].reshape(span, 128)], axis=1
        )

    def window(i, step):
        g = block_at(i + step)
        for m in range(3):
            t = toe[step, m * all_rows : (m + 1) * all_rows, :]
            h = jnp.dot(t, g, preferred_element_type=F32)
            if (i, step) == (0, 0):
                h = h * has_low
            if (i, step) == (NX - 1, 2):
                h = h * has_up
            if step == 1:
                acc[i, m] = h
            else:
                acc[i, m] += h

    def pair_sums(i, j, m):
        z = lax.dot_general(wgt[i, m], block_at(j), NT, preferred_element_type=F32)
        total = None
        for k in range(4):
            a = z[own_e * k : own_e * (k + 1)]
            b = z[own_e * (k + 4) : own_e * (k + 5)]
            lo, hi = turn(a[:, :128] + b[:, 128:], a[:, 128:] + b[:, :128], span - 32 * k)
            total = (lo, hi) if total is None else (total[0] + lo, total[1] + hi)
        return total

    row8 = lax.broadcasted_iota(jnp.int32, (8, 128), 0)

    def diagonals(a, b):
        total = None
        for at in range(0, own_e, 8):
            x = pltpu.roll(a[at : at + 8], (127 - at) % 128, 1)
            x = x + pltpu.roll(b[at : at + 8], (127 + own_e - at) % 128, 1)
            total = x if total is None else total + x
        for bit in (1, 2, 4):
            total = jnp.where(row8 & bit != 0, pltpu.roll(total, 128 - bit, 1), total)
        return total

    await_ring(gl_r, 1, r_gl)
    spread_rows(1)
    spread_rows(2)
    own_sums, up_sums = [], []
    for m in range(3):
        x, y = pair_sums(0, 1, m), pair_sums(1, 2, m)
        own_sums.append([x[side] + y[side] for side in range(2)])
        up_sums.append(pair_sums(0, 2, m))
    for a in range(moms):
        landed(gl_r.at[3, a], r_gl.at[3, a])
    spread_rows(3)
    scale = 1.0 / (NO * np.sqrt(np.float32(momenta * ens * own_e)))
    found = [[], []]
    for m in range(3):
        last = pair_sums(1, 3, m)
        for side in range(2):
            a = jnp.where(spot > row, own_sums[m][side], 0.0)
            b = jnp.where(spot <= row, up_sums[m][side] + last[side] * has_up, 0.0)
            found[side].append(jnp.sum(diagonals(a, b), axis=0, keepdims=True) * scale)
    part[...] = jnp.concatenate(found[0] + found[1] + [jnp.zeros((2, 128), F32)], axis=0)
    got_z[iz] = part[...]
    for rel in range(1, nz):
        send(remote(part, got_z.at[iz], s_z.at[rel], r_z.at[iz], me, z_of[rel]))

    window(0, 1)
    window(1, 1)
    window(0, 2)
    window(1, 0)
    window(1, 2)
    for a in range(moms):
        landed(gl_r.at[0, a], r_gl.at[0, a])
    spread_rows(0)
    window(0, 0)
    for i in range(NX):
        se = None
        for m in range(3):
            hi, lo = split(acc[i, m])
            for x, y in ((hi, kr_hi), (lo, kr_hi), (hi, kr_lo)):
                term = jnp.dot(x, y[m], preferred_element_type=F32)
                se = term if se is None else se + term
        for a in range(moms):
            x = se[rows * a : rows * (a + 1)]
            se_t[i, a, :rows, :] = x[:, :MAIN].astype(BF)
            se_t[i, a, rows:, :] = pack_tail(x[:, MAIN:]).astype(BF)
    for i, (rx, rm) in enumerate(mates):
        if i:
            send(remote(
                se_t.at[ix_of[rx], mom_of[rm]], se_r.at[pair], s_se.at[i], r_se.at[pair],
                mom_of[rm], ring * NX + ix_of[rx],
            ))
    se_r[pair] = se_t[ix, me]

    for rel in range(1, nz):
        at = lax.rem(iz + rel, nz)
        landed(got_z.at[at], r_z.at[at])
    total = got_z[0]
    for z in range(1, nz):
        total = total + got_z[z]
    plane[...] = total
    got_p[iy, pair] = total
    for i, (ry, rx, rm) in enumerate(flats):
        send(remote(
            plane, got_p.at[iy, pair], s_p.at[i], r_p.at[iy, pair],
            mom_of[rm], (y_of[ry] * nz + iz) * NX + ix_of[rx],
        ))

    for i, (rx, rm) in enumerate(mates):
        if i:
            at = mom_of[rm] * NX + ix_of[rx]
            landed(se_r.at[at], r_se.at[at])
    for p in range(pairs):
        at = pl.ds(p, rows, stride=pairs)
        rows_f.at[0][at, :] = se_r[p, :rows, :128].astype(F32)
        rows_f.at[1][at, :] = se_r[p, :rows, 128:].astype(F32)
        tails = unpack_tail(se_r[p, rows:, :].astype(F32))
        rows_f.at[2][at, :] = jnp.concatenate(tails, axis=0)
    whole = jnp.concatenate([rows_f[0], rows_f[1], rows_f[2, :, :TAIL]], axis=1)
    se_ref[...] = whole.reshape(own_k, own_e, pairs, 2 * NN).astype(BF)

    for ry, rx, rm in flats:
        at = (y_of[ry], mom_of[rm] * NX + ix_of[rx])
        landed(got_p.at[at[0], at[1]], r_p.at[at[0], at[1]])
    own_q = momenta // moms
    for p in range(pairs):
        total = got_p[0, p]
        for y in range(1, ny):
            total = total + got_p[y, p]
        x = jnp.where(me >= moms // 2, total[3:6], total[0:3])
        x = jnp.where(lax.rem(me, 2) == 1, pltpu.roll(x, 64, 1), x)
        for q in range(own_q):
            y = pltpu.roll(x, 128 - 32 * q, 1) if q else x
            for m in range(3):
                pol_ref[q, m, p, :] = y[m, :window_n]
    for copy in sent:
        copy.wait_send()


def deliver(se_ref, pol_ref, se_out, pol_out, sems):
    copies = [
        pltpu.make_async_copy(se_ref, se_out, sems.at[0]),
        pltpu.make_async_copy(pol_ref, pol_out, sems.at[1]),
    ]
    for copy in copies:
        copy.start()
    for copy in copies:
        copy.wait()


def body(green_less, green_greater, derivative, neighbours, phonon):
    own_k, own_e, pairs, width = green_less.shape
    momenta, window_n = phonon.shape[1], phonon.shape[2]
    moms, ens = lax.axis_size("mom"), lax.axis_size("en")
    nz = min(8, ens // NX)
    ny = ens // (nz * NX)
    dims = (moms, ens, ny, nz, own_k, own_e, pairs, momenta, window_n)
    mates = moms * NX
    span = 32 * momenta
    rows = own_k * own_e
    all_rows = momenta * own_e
    sent = rows + 8
    constants = [jnp.asarray(t, BF) for t in tables()]
    dma = pltpu.SemaphoreType.DMA
    operands = [
        green_less, green_greater, derivative.transpose(1, 0, 2), neighbours,
        phonon.transpose(0, 1, 3, 4, 2), *constants,
    ]
    order = [0, 1, 2, 4, 5, 6, 7, 8, 9]
    near = [pltpu.VMEM(operands[i].shape, operands[i].dtype) for i in order]
    near.insert(3, pltpu.SMEM(neighbours.shape, neighbours.dtype))
    self_energy, pol = pl.pallas_call(
        functools.partial(kernel, dims),
        out_shape=(
            pltpu.VMEM((own_k, own_e, pairs, width), BF),
            pltpu.VMEM((momenta // moms, 3, pairs, window_n), F32),
        ),
        in_specs=[pl.BlockSpec(memory_space=pl.ANY)] * len(operands),
        out_specs=(pl.BlockSpec(memory_space=pltpu.VMEM),) * 2,
        scratch_shapes=near + [
            pltpu.VMEM((3, rows * pairs, 128), F32),
            pltpu.VMEM((pairs, sent, MAIN), BF),
            pltpu.VMEM((pairs, sent, MAIN), BF),
            pltpu.VMEM((4, moms, sent, MAIN), BF),
            pltpu.VMEM((NX, moms, sent, MAIN), BF),
            pltpu.VMEM((4, momenta, 32, MAIN), BF),
            pltpu.VMEM((4, momenta, 32, 128), BF),
            pltpu.VMEM((NX, all_rows, 128), BF),
            pltpu.VMEM((4, 2, 3 * pairs, 128), F32),
            pltpu.VMEM((3, 3 * all_rows, span), BF),
            pltpu.VMEM((3, WIDE, WIDE), BF),
            pltpu.VMEM((3, WIDE, WIDE), BF),
            pltpu.VMEM((NX, 3, all_rows, WIDE), BF),
            pltpu.VMEM((NX, 3, all_rows, WIDE), F32),
            pltpu.VMEM((NX, moms, sent, MAIN), BF),
            pltpu.VMEM((pairs, sent, MAIN), BF),
            pltpu.VMEM((8, 128), F32),
            pltpu.VMEM((nz, 8, 128), F32),
            pltpu.VMEM((8, 128), F32),
            pltpu.VMEM((ny, pairs, 8, 128), F32),
            dma((len(operands),)), dma((mates,)), dma((NX, moms)), dma((mates,)), dma((mates,)),
            dma((4, moms)), dma((mates,)), dma((pairs,)), dma((nz,)), dma((nz,)),
            dma((ny * mates,)), dma((ny, pairs)),
        ],
        compiler_params=pltpu.CompilerParams(collective_id=0, has_side_effects=True),
    )(*operands)
    self_energy = pltpu.with_memory_space_constraint(self_energy, pltpu.VMEM)
    pol = pltpu.with_memory_space_constraint(pol, pltpu.VMEM)
    self_energy, pol = pl.pallas_call(
        deliver,
        out_shape=tuple(jax.ShapeDtypeStruct(x.shape, x.dtype) for x in (self_energy, pol)),
        in_specs=[pl.BlockSpec(memory_space=pltpu.VMEM)] * 2,
        out_specs=(pl.BlockSpec(memory_space=pl.ANY),) * 2,
        scratch_shapes=[dma((2,))],
        compiler_params=pltpu.CompilerParams(vmem_limit_bytes=16 << 20),
    )(self_energy, pol)
    return self_energy, pol.transpose(0, 3, 1, 2)


def solution(mesh):
    return jax.shard_map(
        body,
        mesh=mesh,
        in_specs=(P("mom", "en", None, None), P("mom", "en", None, None), P(), P(), P()),
        out_specs=(P("mom", "en", None, None), P("mom", None, None, None)),
        check_vma=False,
    )
```

profile of v0, /device:TPU:1, one launch (start us, length us, event | category | flops | bytes accessed | tf_op | source)
XLA Modules:
  0.0 36.2 jit_solution(12044155781093160461)
XLA Ops:
  0.6 34.8 %shard_map.113 = (bf16[2,24,8,288]{3,2,1,0:T(8,128)(2,1)S(1)}, f32[2,3,8,24]{3,2,1,0:T(8,128)S(1)}) custom-call(bf16[2,24,8,288]{3,2,1,0:T(8,128)(2,1)} %gl_hbm.1, bf16[2,24,8,288]{3,2,1,0:T(8,128)(2,1)} %gg_hbm.1, f32[3,2,144]{2,1,0:T(2,128)} %bitcast.4, s32[2,4]{1,0:T(2,128)} %nb_hbm.1, bf16[2,8,3,8,24]{4,3,2,1,0:T(8,128)(2,1)} %bitcast.3, ...), custom_call_target="tpu_custom_call" | custom-call | tf_op jit(solution)/shard_map/pallas_call | solution.py:472
  35.5 0.7 %shard_map.114 = (bf16[2,24,8,288]{3,2,1,0:T(8,128)(2,1)}, f32[2,3,8,24]{3,2,1,0:T(8,128)}) custom-call(bf16[2,24,8,288]{3,2,1,0:T(8,128)(2,1)S(1)} %get-tuple-element.6.se_ref, f32[2,3,8,24]{3,2,1,0:T(8,128)S(1)} %get-tuple-element.7.pol_ref), custom_call_target="tpu_custom_call" | custom-call | tf_op jit(solution)/shard_map/pallas_call | solution.py:509
where the time goes:
time: 36.3 us; the launch traced here: 36.2 us
  Pallas kernels  35.6 us (98%)
  between operations  0.64 us (2%)
    pallas_call x1, Pallas kernels, body(): pl.pallas_call(functools.partial(kernel, dims), out_shape=(pltpu.VMEM((ow...  34.8 us
    pallas_call x1, Pallas kernels, body(): pl.pallas_call(deliver, out_shape=tuple((jax.ShapeDtypeStruct(x.shape, x....  0.74 us

commit v1 on v0

--- a/solution.py
+++ b/solution.py
@@ -23,18 +23,19 @@
 
 def tables():
     r = np.arange(NN)
-    col = np.arange(2 * NN)
-    sub = col % NN
-    rows_s = (r[None, :] % NO == r[:, None] // NO).astype(np.float32)
-    rows_t = (r[None, :] % NO == r[:, None] % NO).astype(np.float32)
-    cols_i = np.zeros((NN, WIDE), np.float32)
-    cols_u = np.zeros((NN, WIDE), np.float32)
-    cols_i[:, : 2 * NN] = r[:, None] // NO == sub[None, :] // NO
-    cols_u[:, : 2 * NN] = r[:, None] // NO == sub[None, :] % NO
-    swap = np.zeros((WIDE, WIDE), np.float32)
-    flipped = (col // NN) * NN + (sub % NO) * NO + sub // NO
-    swap[flipped, col] = np.where(col < NN, 1.0, -1.0)
-    return rows_s, rows_t, cols_i, cols_u, swap
+    first, second = r // NO, r % NO
+    rows = np.zeros((4, NN, NN), np.float32)
+    cols = np.zeros((4, NN, WIDE), np.float32)
+    sub = np.arange(2 * NN) % NN
+    for at, (of_row, own, of_col, other) in enumerate((
+        (second, first, first, sub // NO),
+        (second, second, first, sub % NO),
+        (first, second, second, sub // NO),
+        (first, first, second, sub % NO),
+    )):
+        rows[at] = of_row[None, :] == own[:, None]
+        cols[at, :, : 2 * NN] = of_col[:, None] == other[None, :]
+    return rows, cols
 
 
 def split(x):
@@ -44,10 +45,11 @@
 
 def kernel(
     dims,
-    gl_hbm, gg_hbm, der_hbm, nb_hbm, ph_hbm, rs_hbm, rt_hbm, ci_hbm, cu_hbm, swap_hbm,
+    gl_hbm, gg_hbm, der_hbm, nb_hbm, ph_hbm, rt_hbm, ct_hbm,
     se_ref, pol_ref,
-    gl_in, gg_in, der_ref, nb_ref, ph_ref, rs_ref, rt_ref, ci_ref, cu_ref, swap_ref,
-    rows_f, gl_t, gg_t, gl_r, gg_r, gl, gl_tail, gg_tail, coef, toe, kr_hi, kr_lo, wgt, acc,
+    gl_in, gg_in, der_ref, nb_ref, ph_ref, rt_ref, ct_ref,
+    rows_f, gl_t, gg_t, gl_r, gg_r, gl, gl_tail, gg_tail, coef, toe, ks_hi, ks_lo, ks_tail, kw,
+    wgt, wgt_tail, acc, acc_tail,
     se_t, se_r, part, got_z, plane, got_p,
     loads, s_gg, r_gg, s_own, s_halo, r_gl, s_se, r_se, s_z, r_z, s_p, r_p,
 ):
@@ -64,8 +66,8 @@
     above_ring, below_ring = lax.rem(ring + 1, rings), lax.rem(ring + rings - 1, rings)
     pair = me * NX + ix
 
-    hbm = (gg_hbm, gl_hbm, ph_hbm, der_hbm, nb_hbm, rs_hbm, rt_hbm, ci_hbm, cu_hbm, swap_hbm)
-    near = (gg_in, gl_in, ph_ref, der_ref, nb_ref, rs_ref, rt_ref, ci_ref, cu_ref, swap_ref)
+    hbm = (gg_hbm, gl_hbm, ph_hbm, der_hbm, nb_hbm, rt_hbm, ct_hbm)
+    near = (gg_in, gl_in, ph_ref, der_ref, nb_ref, rt_ref, ct_ref)
     fetch = [pltpu.make_async_copy(a, b, loads.at[i]) for i, (a, b) in enumerate(zip(hbm, near))]
     for copy in fetch:
         copy.start()
@@ -179,12 +181,13 @@
                 landed(buffer.at[at, mom_of[rm]], sems.at[at, mom_of[rm]])
 
     gl[:, :, own_e:, :] = jnp.zeros((4, momenta, 32 - own_e, MAIN), BF)
-    gl_tail[:, :, own_e:, :] = jnp.zeros((4, momenta, 32 - own_e, 128), BF)
+    gl_tail[...] = jnp.zeros((3, momenta, 32, 128), BF)
 
     for copy in fetch[2:]:
         copy.wait()
 
     first_part = lax.broadcasted_iota(jnp.int32, (NN, WIDE), 1) < NN
+    pair_lane = lax.broadcasted_iota(jnp.int32, (NN, 128), 1)
 
     def expand(row, rows_of, cols_of):
         hi, lo = split(row)
@@ -199,16 +202,43 @@
 
     cut = MAIN - NN
     other = nb_ref[pair // NB, lax.rem(pair, NB)]
+    main = 3 * MAIN
+    ks_hi[main + 3 * TAIL :, :] = jnp.zeros((128 - 3 * TAIL, MAIN), BF)
+    ks_lo[main + 3 * TAIL :, :] = jnp.zeros((128 - 3 * TAIL, MAIN), BF)
+    ks_tail[...] = jnp.zeros((main + 128, 128), BF)
+    kw[2 * MAIN :, :] = jnp.zeros((128, main + 128), BF)
+    kw[:, main + 96 :] = jnp.zeros((2 * MAIN + 128, 32), BF)
     for m in range(3):
-        left = expand(block_of(m, pair // NB), rs_ref[...], ci_ref[...])
-        right = expand(block_of(m, other), rt_ref[...], cu_ref[...])
-        both = left * right
+        left, right = block_of(m, pair // NB), block_of(m, other)
+        both = expand(left, rt_ref[0], ct_ref[0]) * expand(right, rt_ref[1], ct_ref[1])
+        tops = split(jnp.where(first_part, both, 0.0))
+        lows = split(jnp.where(first_part, 0.0, both))
+        at = MAIN * m
+        tail_at = main + TAIL * m
+        for dst, top, low in zip((ks_hi, ks_lo), tops, lows):
+            dst[at : at + NN, :] = top[:, :MAIN]
+            dst[at + NN : at + MAIN, :] = low[:cut, :MAIN]
+            dst[tail_at : tail_at + TAIL, :] = low[cut:, :MAIN]
+        last = jnp.where(first_part, 0.0, both)[:, MAIN:]
+        hi = last.astype(BF).astype(F32)
+        last = jnp.where(pair_lane < TAIL, hi, pltpu.roll(last - hi, TAIL, 1)).astype(BF)
+        ks_tail[at + NN : at + MAIN, :] = last[:cut]
+        ks_tail[tail_at : tail_at + TAIL, :] = last[cut:]
+        both = expand(left, rt_ref[2], ct_ref[2]) * expand(right, rt_ref[3], ct_ref[3])
         top = jnp.where(first_part, both, 0.0)
-        low = jnp.where(first_part, 0.0, both)
-        for dst, a, b in zip((kr_hi, kr_lo), split(top), split(low)):
-            dst[m, :NN, :] = a
-            dst[m, NN : 2 * NN, :] = b
-            dst[m, 2 * NN :, :] = jnp.zeros((WIDE - 2 * NN, WIDE), BF)
+        low = jnp.where(first_part, 0.0, -both)
+        shift = lambda x: pltpu.roll(x[:, MAIN:], TAIL * m, 1) if m else x[:, MAIN:]
+        lane_at = slice(main + TAIL * m, main + TAIL * (m + 1))
+        last = split(shift(low))
+        for half, (x, y, z) in enumerate(zip(split(top), split(low), last)):
+            z = z[:, TAIL * m : TAIL * (m + 1)]
+            row_at, rest = MAIN * half, 2 * MAIN + TAIL * half
+            kw[row_at : row_at + NN, at : at + MAIN] = x[:, :MAIN]
+            kw[row_at + NN : row_at + MAIN, at : at + MAIN] = y[:cut, :MAIN]
+            kw[rest : rest + TAIL, at : at + MAIN] = y[cut:, :MAIN]
+            kw[row_at : row_at + NN, lane_at] = jnp.zeros((NN, TAIL), BF)
+            kw[row_at + NN : row_at + MAIN, lane_at] = z[:cut]
+            kw[rest : rest + TAIL, lane_at] = z[cut:]
 
     lane = lax.broadcasted_iota(jnp.int32, (own_e, 128), 1)
     row = lax.broadcasted_iota(jnp.int32, (own_e, 128), 0)
@@ -275,51 +305,77 @@
 
     has_low = (ring > 0).astype(F32)
     has_up = (ring < rings - 1).astype(F32)
+    tail_lane = lax.broadcasted_iota(jnp.int32, (all_rows, 128), 1)
+
+    def moved(x, source, target):
+        n = (target - source) % 128
+        x = pltpu.roll(x, n, 1) if n else x
+        return jnp.where((tail_lane >= target) & (tail_lane < target + TAIL), x, 0.0)
 
     await_ring(gg_r, 0, r_gg)
     for i in range(NX):
         for a in range(moms):
             tails = unpack_tail(gg_r[i, a, rows:, :].astype(F32))
+            tails = [x + pltpu.roll(x, TAIL, 1) for x in tails]
             gg_tail[i, rows * a : rows * (a + 1), :] = jnp.concatenate(tails, axis=0).astype(BF)
-        block = jnp.concatenate(
-            [gg_r[i, :, :rows, :].reshape(all_rows, MAIN), gg_tail[i]], axis=1
-        )
-        swapped = jnp.dot(block, swap_ref[...], preferred_element_type=F32).astype(BF)
+        block = gg_r[i, :, :rows, :].reshape(all_rows, MAIN)
+        block = jnp.concatenate([block, block, gg_tail[i]], axis=1)
         for m in range(3):
-            w = lax.dot_general(swapped, kr_hi[m], NT, preferred_element_type=F32)
-            w = w + lax.dot_general(swapped, kr_lo[m], NT, preferred_element_type=F32)
+            w = jnp.dot(block, kw[:, MAIN * m : MAIN * (m + 1)], preferred_element_type=F32)
             wgt[i, m] = w.astype(BF)
-
-    def spread_rows(j):
+        w = jnp.dot(block, kw[:, main:], preferred_element_type=F32)
+        for m in range(3):
+            wgt_tail[i, m] = moved(w, TAIL * m, TAIL * i).astype(BF)
+
+    def spread_rows(j, factor=None):
         for a in range(moms):
             for k in range(own_k):
-                gl[j, own_k * a + k, :own_e, :] = gl_r[j, a, own_e * k : own_e * (k + 1), :]
+                x = gl_r[j, a, own_e * k : own_e * (k + 1), :]
+                if factor is not None:
+                    x = (x.astype(F32) * factor).astype(BF)
+                gl[j, own_k * a + k, :own_e, :] = x
             tails = unpack_tail(gl_r[j, a, rows:, :].astype(F32))
             for k in range(own_k):
                 x = jnp.concatenate(tails[3 * k : 3 * (k + 1)], axis=0)
-                gl_tail[j, own_k * a + k, :own_e, :] = x.astype(BF)
-
-    def block_at(j):
-        return jnp.concatenate(
-            [gl[j].reshape(span, MAIN), gl_tail[j].reshape(span, 128)], axis=1
-        )
-
-    def window(i, step):
-        g = block_at(i + step)
+                if factor is not None:
+                    x = x * factor
+                at = own_k * a + k
+                if j < 3:
+                    gl_tail[j, at, :own_e, :TAIL] = x[:, :TAIL].astype(BF)
+                if j > 0:
+                    x = pltpu.roll(x, TAIL, 1)[:, TAIL : 2 * TAIL]
+                    gl_tail[j - 1, at, :own_e, TAIL : 2 * TAIL] = x.astype(BF)
+
+    def window(i, step, first=False):
         for m in range(3):
             t = toe[step, m * all_rows : (m + 1) * all_rows, :]
-            h = jnp.dot(t, g, preferred_element_type=F32)
-            if (i, step) == (0, 0):
-                h = h * has_low
-            if (i, step) == (NX - 1, 2):
-                h = h * has_up
-            if step == 1:
+            h = jnp.dot(t, gl[i + step].reshape(span, MAIN), preferred_element_type=F32)
+            if first:
                 acc[i, m] = h
             else:
                 acc[i, m] += h
 
-    def pair_sums(i, j, m):
-        z = lax.dot_general(wgt[i, m], block_at(j), NT, preferred_element_type=F32)
+    def window_tail(step, first=False):
+        for m in range(3):
+            t = toe[step, m * all_rows : (m + 1) * all_rows, :]
+            h = jnp.dot(t, gl_tail[step].reshape(span, 128), preferred_element_type=F32)
+            if first:
+                acc_tail[m] = h
+            else:
+                acc_tail[m] += h
+
+    def pair_sums(m, edges, tail_at):
+        z = None
+        tail = None
+        for i, j in edges:
+            x = lax.dot_general(
+                wgt[i, m], gl[j].reshape(span, MAIN), NT, preferred_element_type=F32
+            )
+            z = x if z is None else z + x
+            tail = wgt_tail[i, m] if tail is None else tail + wgt_tail[i, m]
+        z = z + lax.dot_general(
+            tail, gl_tail[tail_at].reshape(span, 128), NT, preferred_element_type=F32
+        )
         total = None
         for k in range(4):
             a = z[own_e * k : own_e * (k + 1)]
@@ -343,43 +399,47 @@
     await_ring(gl_r, 1, r_gl)
     spread_rows(1)
     spread_rows(2)
-    own_sums, up_sums = [], []
-    for m in range(3):
-        x, y = pair_sums(0, 1, m), pair_sums(1, 2, m)
-        own_sums.append([x[side] + y[side] for side in range(2)])
-        up_sums.append(pair_sums(0, 2, m))
+    own_sums = [pair_sums(m, ((0, 1), (1, 2)), 1) for m in range(3)]
+    up_sums = [pair_sums(m, ((0, 2),), 2) for m in range(3)]
+    window(0, 1, True)
+    window(1, 1, True)
+    window_tail(1, True)
+    window(0, 2)
+    window(1, 0)
     for a in range(moms):
         landed(gl_r.at[3, a], r_gl.at[3, a])
-    spread_rows(3)
+    spread_rows(3, has_up)
     scale = 1.0 / (NO * np.sqrt(np.float32(momenta * ens * own_e)))
     found = [[], []]
     for m in range(3):
-        last = pair_sums(1, 3, m)
+        last = pair_sums(m, ((1, 3),), 2)
         for side in range(2):
             a = jnp.where(spot > row, own_sums[m][side], 0.0)
-            b = jnp.where(spot <= row, up_sums[m][side] + last[side] * has_up, 0.0)
+            b = jnp.where(spot <= row, up_sums[m][side] + last[side], 0.0)
             found[side].append(jnp.sum(diagonals(a, b), axis=0, keepdims=True) * scale)
     part[...] = jnp.concatenate(found[0] + found[1] + [jnp.zeros((2, 128), F32)], axis=0)
     got_z[iz] = part[...]
     for rel in range(1, nz):
         send(remote(part, got_z.at[iz], s_z.at[rel], r_z.at[iz], me, z_of[rel]))
 
-    window(0, 1)
-    window(1, 1)
-    window(0, 2)
-    window(1, 0)
     window(1, 2)
+    window_tail(2)
     for a in range(moms):
         landed(gl_r.at[0, a], r_gl.at[0, a])
-    spread_rows(0)
+    spread_rows(0, has_low)
     window(0, 0)
+    window_tail(0)
     for i in range(NX):
-        se = None
-        for m in range(3):
-            hi, lo = split(acc[i, m])
-            for x, y in ((hi, kr_hi), (lo, kr_hi), (hi, kr_lo)):
-                term = jnp.dot(x, y[m], preferred_element_type=F32)
-                se = term if se is None else se + term
+        tail = sum(moved(acc_tail[m], TAIL * i, TAIL * m) for m in range(3))
+        hi, lo = zip(*[split(x) for x in (acc[i, 0], acc[i, 1], acc[i, 2], tail)])
+        hi, lo = jnp.concatenate(hi, axis=1), jnp.concatenate(lo, axis=1)
+        se = jnp.dot(hi, ks_hi[...], preferred_element_type=F32)
+        se = se + jnp.dot(lo, ks_hi[...], preferred_element_type=F32)
+        se = se + jnp.dot(hi, ks_lo[...], preferred_element_type=F32)
+        tail = jnp.dot(hi, ks_tail[...], preferred_element_type=F32)
+        tail = tail + jnp.dot(lo, ks_tail[...], preferred_element_type=F32)
+        tail = tail + pltpu.roll(tail, 128 - TAIL, 1)
+        se = jnp.concatenate([se, tail], axis=1)
         for a in range(moms):
             x = se[rows * a : rows * (a + 1)]
             se_t[i, a, :rows, :] = x[:, :MAIN].astype(BF)
@@ -398,11 +458,12 @@
     total = got_z[0]
     for z in range(1, nz):
         total = total + got_z[z]
-    plane[...] = total
-    got_p[iy, pair] = total
+    for half in range(2):
+        plane[half, :3] = total[3 * half : 3 * (half + 1)]
+    got_p[iy, pair] = plane[me // (moms // 2)]
     for i, (ry, rx, rm) in enumerate(flats):
         send(remote(
-            plane, got_p.at[iy, pair], s_p.at[i], r_p.at[iy, pair],
+            plane.at[mom_of[rm] // (moms // 2)], got_p.at[iy, pair], s_p.at[i], r_p.at[iy, pair],
             mom_of[rm], (y_of[ry] * nz + iz) * NX + ix_of[rx],
         ))
 
@@ -427,8 +488,7 @@
         total = got_p[0, p]
         for y in range(1, ny):
             total = total + got_p[y, p]
-        x = jnp.where(me >= moms // 2, total[3:6], total[0:3])
-        x = jnp.where(lax.rem(me, 2) == 1, pltpu.roll(x, 64, 1), x)
+        x = jnp.where(lax.rem(me, 2) == 1, pltpu.roll(total, 64, 1), total)
         for q in range(own_q):
             y = pltpu.roll(x, 128 - 32 * q, 1) if q else x
             for m in range(3):
@@ -466,7 +526,7 @@
         green_less, green_greater, derivative.transpose(1, 0, 2), neighbours,
         phonon.transpose(0, 1, 3, 4, 2), *constants,
     ]
-    order = [0, 1, 2, 4, 5, 6, 7, 8, 9]
+    order = [0, 1, 2, 4, 5, 6]
     near = [pltpu.VMEM(operands[i].shape, operands[i].dtype) for i in order]
     near.insert(3, pltpu.SMEM(neighbours.shape, neighbours.dtype))
     self_energy, pol = pl.pallas_call(
@@ -484,20 +544,24 @@
             pltpu.VMEM((4, moms, sent, MAIN), BF),
             pltpu.VMEM((NX, moms, sent, MAIN), BF),
             pltpu.VMEM((4, momenta, 32, MAIN), BF),
-            pltpu.VMEM((4, momenta, 32, 128), BF),
+            pltpu.VMEM((3, momenta, 32, 128), BF),
             pltpu.VMEM((NX, all_rows, 128), BF),
             pltpu.VMEM((4, 2, 3 * pairs, 128), F32),
             pltpu.VMEM((3, 3 * all_rows, span), BF),
-            pltpu.VMEM((3, WIDE, WIDE), BF),
-            pltpu.VMEM((3, WIDE, WIDE), BF),
-            pltpu.VMEM((NX, 3, all_rows, WIDE), BF),
-            pltpu.VMEM((NX, 3, all_rows, WIDE), F32),
+            pltpu.VMEM((3 * MAIN + 128, MAIN), BF),
+            pltpu.VMEM((3 * MAIN + 128, MAIN), BF),
+            pltpu.VMEM((3 * MAIN + 128, 128), BF),
+            pltpu.VMEM((2 * MAIN + 128, 3 * MAIN + 128), BF),
+            pltpu.VMEM((NX, 3, all_rows, MAIN), BF),
+            pltpu.VMEM((NX, 3, all_rows, 128), BF),
+            pltpu.VMEM((NX, 3, all_rows, MAIN), F32),
+            pltpu.VMEM((3, all_rows, 128), F32),
             pltpu.VMEM((NX, moms, sent, MAIN), BF),
             pltpu.VMEM((pairs, sent, MAIN), BF),
             pltpu.VMEM((8, 128), F32),
             pltpu.VMEM((nz, 8, 128), F32),
-            pltpu.VMEM((8, 128), F32),
-            pltpu.VMEM((ny, pairs, 8, 128), F32),
+            pltpu.VMEM((2, 4, 128), F32),
+            pltpu.VMEM((ny, pairs, 4, 128), F32),
             dma((len(operands),)), dma((mates,)), dma((NX, moms)), dma((mates,)), dma((mates,)),
             dma((4, moms)), dma((mates,)), dma((pairs,)), dma((nz,)), dma((nz,)),
             dma((ny * mates,)), dma((ny, pairs)),

time: 36.3 us -> 34.8 us (0.959)
  Pallas kernels: 35.6 us -> 34.1 us
    pallas_call x1, Pallas kernels: 34.8 us -> 33.3 us  [body(): pl.pallas_call(functools.partial(kernel, dims), out_shape=(pltpu.VMEM((ow...]
where the time goes in v1:
time: 34.8 us; the launch traced here: 34.7 us
  Pallas kernels  34.1 us (98%)
  between operations  0.64 us (2%)
    pallas_call x1, Pallas kernels, body(): pl.pallas_call(functools.partial(kernel, dims), out_shape=(pltpu.VMEM((ow...  33.3 us
    pallas_call x1, Pallas kernels, body(): pl.pallas_call(deliver, out_shape=tuple((jax.ShapeDtypeStruct(x.shape, x....  0.74 us

profile of v1, /device:TPU:1, one launch (start us, length us, event | category | flops | bytes accessed | tf_op | source)
XLA Modules:
  0.0 34.7 jit_solution(5001499067129230166)
XLA Ops:
  0.6 33.3 %shard_map.86 = (bf16[2,24,8,288]{3,2,1,0:T(8,128)(2,1)S(1)}, f32[2,3,8,24]{3,2,1,0:T(8,128)S(1)}) custom-call(bf16[2,24,8,288]{3,2,1,0:T(8,128)(2,1)} %gl_hbm.1, bf16[2,24,8,288]{3,2,1,0:T(8,128)(2,1)} %gg_hbm.1, f32[3,2,144]{2,1,0:T(2,128)} %bitcast.4, s32[2,4]{1,0:T(2,128)} %nb_hbm.1, bf16[2,8,3,8,24]{4,3,2,1,0:T(8,128)(2,1)} %bitcast.3, ...), custom_call_target="tpu_custom_call" | custom-call | tf_op jit(solution)/shard_map/pallas_call | solution.py:532
  34.0 0.7 %shard_map.87 = (bf16[2,24,8,288]{3,2,1,0:T(8,128)(2,1)}, f32[2,3,8,24]{3,2,1,0:T(8,128)}) custom-call(bf16[2,24,8,288]{3,2,1,0:T(8,128)(2,1)S(1)} %get-tuple-element.6.se_ref, f32[2,3,8,24]{3,2,1,0:T(8,128)S(1)} %get-tuple-element.7.pol_ref), custom_call_target="tpu_custom_call" | custom-call | tf_op jit(solution)/shard_map/pallas_call | solution.py:573

commit v2 on v1

--- a/solution.py
+++ b/solution.py
@@ -66,8 +66,8 @@
     above_ring, below_ring = lax.rem(ring + 1, rings), lax.rem(ring + rings - 1, rings)
     pair = me * NX + ix
 
-    hbm = (gg_hbm, gl_hbm, ph_hbm, der_hbm, nb_hbm, rt_hbm, ct_hbm)
-    near = (gg_in, gl_in, ph_ref, der_ref, nb_ref, rt_ref, ct_ref)
+    hbm = (gl_hbm, gg_hbm, ph_hbm, der_hbm, nb_hbm, rt_hbm, ct_hbm)
+    near = (gl_in, gg_in, ph_ref, der_ref, nb_ref, rt_ref, ct_ref)
     fetch = [pltpu.make_async_copy(a, b, loads.at[i]) for i, (a, b) in enumerate(zip(hbm, near))]
     for copy in fetch:
         copy.start()
@@ -79,14 +79,17 @@
             barrier, inc=1, device_id={"mom": mom_at, "en": en_at}, device_id_type=MESH
         )
 
-    mom_of = [me] + [lax.rem(me + rel, moms) for rel in range(1, moms)]
+    core, far = lax.rem(me, 2), me // 2
+    mom_of = [
+        (far if rm < 2 else 1 - far) * 2 + (1 - core if rm % 2 else core) for rm in range(moms)
+    ]
     ix_of = [ix, 1 - ix]
-    mates = [(rx, rm) for rx in range(NX) for rm in range(moms)]
+    mates = [(0, 0)] + [(0, 2), (0, 3), (1, 0), (1, 1), (1, 2), (1, 3), (0, 1)]
     for rx, rm in mates:
         if rx or rm:
             greet(mom_of[rm], ring * NX + ix_of[rx])
-        greet(mom_of[rm], above_ring * NX + ix_of[rx])
-        greet(mom_of[rm], below_ring * NX + ix_of[rx])
+    greet(me, above_ring * NX + ix)
+    greet(me, below_ring * NX + ix)
     z_of = [(iy * nz + lax.rem(iz + rel, nz)) * NX + ix for rel in range(nz)]
     for rel in range(1, nz):
         greet(me, z_of[rel])
@@ -95,7 +98,7 @@
     for ry, rx, rm in flats:
         if ry:
             greet(mom_of[rm], (y_of[ry] * nz + iz) * NX + ix_of[rx])
-    greeted = 3 * len(mates) - 1 + nz - 1 + (ny - 1) * len(mates)
+    greeted = len(mates) + 1 + nz - 1 + (ny - 1) * len(mates)
 
     lane8 = lax.broadcasted_iota(jnp.int32, (8, 128), 1)
 
@@ -144,35 +147,24 @@
         copy.start()
         sent.append(copy)
 
+    def to_ring(source, buffer, first, sends, recvs):
+        for i, (rx, rm) in enumerate(mates):
+            if i:
+                to = mom_of[rm] * NX + ix_of[rx]
+                send(remote(
+                    source.at[to], buffer.at[first + ix, me], sends.at[i], recvs.at[first + ix, me],
+                    mom_of[rm], ring * NX + ix_of[rx],
+                ))
+
     fetch[0].wait()
+    by_pair(gl_in, gl_t)
+    pl.semaphore_wait(barrier, greeted)
+    to_ring(gl_t, gl_r, 1, s_own, r_gl)
+    gl_r[1 + ix, me] = gl_t[pair]
+    fetch[1].wait()
     by_pair(gg_in, gg_t)
-    pl.semaphore_wait(barrier, greeted)
-    for i, (rx, rm) in enumerate(mates):
-        if i:
-            to = mom_of[rm] * NX + ix_of[rx]
-            send(remote(
-                gg_t.at[to], gg_r.at[ix, me], s_gg.at[i], r_gg.at[ix, me],
-                mom_of[rm], ring * NX + ix_of[rx],
-            ))
-    fetch[1].wait()
-    by_pair(gl_in, gl_t)
-    for i, (rx, rm) in enumerate(mates):
-        if i:
-            to = mom_of[rm] * NX + ix_of[rx]
-            send(remote(
-                gl_t.at[to], gl_r.at[1 + ix, me], s_own.at[i], r_gl.at[1 + ix, me],
-                mom_of[rm], ring * NX + ix_of[rx],
-            ))
-    slot = 3 - 3 * ix
-    other_ring = lax.rem(ring + rings + 2 * ix - 1, rings)
-    for i, (rx, rm) in enumerate(mates):
-        to = mom_of[rm] * NX + ix_of[rx]
-        send(remote(
-            gl_t.at[to], gl_r.at[slot, me], s_halo.at[i], r_gl.at[slot, me],
-            mom_of[rm], other_ring * NX + ix_of[rx],
-        ))
+    to_ring(gg_t, gg_r, 0, s_gg, r_gg)
     gg_r[ix, me] = gg_t[pair]
-    gl_r[1 + ix, me] = gl_t[pair]
 
     def await_ring(buffer, first, sems):
         for i, (rx, rm) in enumerate(mates):
@@ -303,6 +295,19 @@
                     both = jnp.concatenate([even[side], odd[side]], axis=0)
                     toe[step, at : at + 2 * own_e, 128 * side : 128 * (side + 1)] = both.astype(BF)
 
+    for i, (rx, rm) in enumerate(mates):
+        half, a = ix_of[rx], mom_of[rm]
+        if i:
+            landed(gl_r.at[1 + half, a], r_gl.at[1 + half, a])
+            source = gl_r.at[1 + half, a]
+        else:
+            source = gl_t.at[pair]
+        target = lax.rem(ring + rings + 2 * half - 1, rings)
+        slot = 3 - 3 * half
+        send(remote(
+            source, gl_r.at[slot, a], s_halo.at[i], r_gl.at[slot, a], me, target * NX + ix,
+        ))
+
     has_low = (ring > 0).astype(F32)
     has_up = (ring < rings - 1).astype(F32)
     tail_lane = lax.broadcasted_iota(jnp.int32, (all_rows, 128), 1)
@@ -396,7 +401,6 @@
             total = jnp.where(row8 & bit != 0, pltpu.roll(total, 128 - bit, 1), total)
         return total
 
-    await_ring(gl_r, 1, r_gl)
     spread_rows(1)
     spread_rows(2)
     own_sums = [pair_sums(m, ((0, 1), (1, 2)), 1) for m in range(3)]

time: 34.8 us -> 33.3 us (0.957)
  Pallas kernels: 34.1 us -> 32.5 us
    pallas_call x1, Pallas kernels: 33.3 us -> 31.8 us  [body(): pl.pallas_call(functools.partial(kernel, dims), out_shape=(pltpu.VMEM((ow...]
where the time goes in v2:
time: 33.3 us; the launch traced here: 33.2 us
  Pallas kernels  32.5 us (98%)
  between operations  0.64 us (2%)
    pallas_call x1, Pallas kernels, body(): pl.pallas_call(functools.partial(kernel, dims), out_shape=(pltpu.VMEM((ow...  31.8 us
    pallas_call x1, Pallas kernels, body(): pl.pallas_call(deliver, out_shape=tuple((jax.ShapeDtypeStruct(x.shape, x....  0.74 us

profile of v2, /device:TPU:1, one launch (start us, length us, event | category | flops | bytes accessed | tf_op | source)
XLA Modules:
  0.0 33.2 jit_solution(3630271851919831585)
XLA Ops:
  0.6 31.8 %shard_map.86 = (bf16[2,24,8,288]{3,2,1,0:T(8,128)(2,1)S(1)}, f32[2,3,8,24]{3,2,1,0:T(8,128)S(1)}) custom-call(bf16[2,24,8,288]{3,2,1,0:T(8,128)(2,1)} %gl_hbm.1, bf16[2,24,8,288]{3,2,1,0:T(8,128)(2,1)} %gg_hbm.1, f32[3,2,144]{2,1,0:T(2,128)} %bitcast.4, s32[2,4]{1,0:T(2,128)} %nb_hbm.1, bf16[2,8,3,8,24]{4,3,2,1,0:T(8,128)(2,1)} %bitcast.3, ...), custom_call_target="tpu_custom_call" | custom-call | tf_op jit(solution)/shard_map/pallas_call | solution.py:536
  32.4 0.7 %shard_map.87 = (bf16[2,24,8,288]{3,2,1,0:T(8,128)(2,1)}, f32[2,3,8,24]{3,2,1,0:T(8,128)}) custom-call(bf16[2,24,8,288]{3,2,1,0:T(8,128)(2,1)S(1)} %get-tuple-element.6.se_ref, f32[2,3,8,24]{3,2,1,0:T(8,128)S(1)} %get-tuple-element.7.pol_ref), custom_call_target="tpu_custom_call" | custom-call | tf_op jit(solution)/shard_map/pallas_call | solution.py:577

commit v3 on v2

--- a/solution.py
+++ b/solution.py
@@ -51,7 +51,7 @@
     rows_f, gl_t, gg_t, gl_r, gg_r, gl, gl_tail, gg_tail, coef, toe, ks_hi, ks_lo, ks_tail, kw,
     wgt, wgt_tail, acc, acc_tail,
     se_t, se_r, part, got_z, plane, got_p,
-    loads, s_gg, r_gg, s_own, s_halo, r_gl, s_se, r_se, s_z, r_z, s_p, r_p,
+    loads, s_gg, r_gg, s_own, s_halo, r_gl, s_se, r_se, s_z, r_z, s_p, r_p, first_word, second_word,
 ):
     moms, ens, ny, nz, own_k, own_e, pairs, momenta, window_n = dims
     rows = own_k * own_e
@@ -84,21 +84,27 @@
         (far if rm < 2 else 1 - far) * 2 + (1 - core if rm % 2 else core) for rm in range(moms)
     ]
     ix_of = [ix, 1 - ix]
-    mates = [(0, 0)] + [(0, 2), (0, 3), (1, 0), (1, 1), (1, 2), (1, 3), (0, 1)]
+    mates = [(0, 0)] + [(0, 2), (1, 0), (0, 3), (1, 1), (1, 2), (1, 3), (0, 1)]
     for rx, rm in mates:
         if rx or rm:
             greet(mom_of[rm], ring * NX + ix_of[rx])
     greet(me, above_ring * NX + ix)
     greet(me, below_ring * NX + ix)
     z_of = [(iy * nz + lax.rem(iz + rel, nz)) * NX + ix for rel in range(nz)]
-    for rel in range(1, nz):
-        greet(me, z_of[rel])
     y_of = [lax.rem(iy + ry, ny) for ry in range(ny)]
+    line_of = [(y_of[ry] * nz + iz) * NX + ix for ry in range(ny)]
     flats = [(ry, rx, rm) for ry in range(ny) for rx in range(NX) for rm in range(moms)][1:]
-    for ry, rx, rm in flats:
-        if ry:
-            greet(mom_of[rm], (y_of[ry] * nz + iz) * NX + ix_of[rx])
-    greeted = len(mates) + 1 + nz - 1 + (ny - 1) * len(mates)
+    next_to = [z_of[1], z_of[nz - 1], line_of[1], line_of[ny - 1]]
+    beyond = [z_of[2], z_of[nz - 2], line_of[2]]
+    for to in next_to:
+        greet(me, to)
+    greeted = len(mates) + 1 + len(next_to)
+
+    def tell(word, devices):
+        for to in devices:
+            pl.semaphore_signal(
+                word, inc=1, device_id={"mom": me, "en": to}, device_id_type=MESH
+            )
 
     lane8 = lax.broadcasted_iota(jnp.int32, (8, 128), 1)
 
@@ -159,6 +165,7 @@
     fetch[0].wait()
     by_pair(gl_in, gl_t)
     pl.semaphore_wait(barrier, greeted)
+    tell(first_word, next_to)
     to_ring(gl_t, gl_r, 1, s_own, r_gl)
     gl_r[1 + ix, me] = gl_t[pair]
     fetch[1].wait()
@@ -232,6 +239,9 @@
             kw[row_at + NN : row_at + MAIN, lane_at] = z[:cut]
             kw[rest : rest + TAIL, lane_at] = z[cut:]
 
+    pl.semaphore_wait(first_word, len(next_to))
+    tell(second_word, beyond)
+
     lane = lax.broadcasted_iota(jnp.int32, (own_e, 128), 1)
     row = lax.broadcasted_iota(jnp.int32, (own_e, 128), 0)
     spot = lax.rem(lane, 32)
@@ -295,18 +305,22 @@
                     both = jnp.concatenate([even[side], odd[side]], axis=0)
                     toe[step, at : at + 2 * own_e, 128 * side : 128 * (side + 1)] = both.astype(BF)
 
-    for i, (rx, rm) in enumerate(mates):
-        half, a = ix_of[rx], mom_of[rm]
-        if i:
-            landed(gl_r.at[1 + half, a], r_gl.at[1 + half, a])
-            source = gl_r.at[1 + half, a]
-        else:
-            source = gl_t.at[pair]
-        target = lax.rem(ring + rings + 2 * half - 1, rings)
-        slot = 3 - 3 * half
-        send(remote(
-            source, gl_r.at[slot, a], s_halo.at[i], r_gl.at[slot, a], me, target * NX + ix,
-        ))
+    for half in range(NX):
+        target, slot = ((below_ring, 3), (above_ring, 0))[half]
+        for rm in (0, 1, 2, 3):
+            a = mom_of[rm]
+            if rm:
+                landed(gl_r.at[1 + half, a], r_gl.at[1 + half, a])
+            else:
+                @pl.when(ix != half)
+                def _():
+                    landed(gl_r.at[1 + half, a], r_gl.at[1 + half, a])
+            send(remote(
+                gl_r.at[1 + half, a], gl_r.at[slot, a], s_halo.at[moms * half + rm],
+                r_gl.at[slot, a], me, target * NX + ix,
+            ))
+
+    pl.semaphore_wait(second_word, len(beyond))
 
     has_low = (ring > 0).astype(F32)
     has_up = (ring < rings - 1).astype(F32)
@@ -462,12 +476,16 @@
     total = got_z[0]
     for z in range(1, nz):
         total = total + got_z[z]
-    for half in range(2):
-        plane[half, :3] = total[3 * half : 3 * (half + 1)]
-    got_p[iy, pair] = plane[me // (moms // 2)]
+    swung = pltpu.roll(total, 64, 1)
+    for a in range(moms):
+        at = 3 * (a // 2)
+        low, high = (total, swung) if a % 2 == 0 else (swung, total)
+        plane[a, 0:1] = jnp.where(lane8[:1] < 64, low[at : at + 1], high[at + 1 : at + 2])
+        plane[a, 1:2] = low[at + 2 : at + 3]
+    got_p[iy, pair] = plane[me]
     for i, (ry, rx, rm) in enumerate(flats):
         send(remote(
-            plane.at[mom_of[rm] // (moms // 2)], got_p.at[iy, pair], s_p.at[i], r_p.at[iy, pair],
+            plane.at[mom_of[rm]], got_p.at[iy, pair], s_p.at[i], r_p.at[iy, pair],
             mom_of[rm], (y_of[ry] * nz + iz) * NX + ix_of[rx],
         ))
 
@@ -492,11 +510,11 @@
         total = got_p[0, p]
         for y in range(1, ny):
             total = total + got_p[y, p]
-        x = jnp.where(lax.rem(me, 2) == 1, pltpu.roll(total, 64, 1), total)
         for q in range(own_q):
-            y = pltpu.roll(x, 128 - 32 * q, 1) if q else x
             for m in range(3):
-                pol_ref[q, m, p, :] = y[m, :window_n]
+                at = 64 * (m % 2) + 32 * q
+                y = pltpu.roll(total, 128 - at, 1) if at else total
+                pol_ref[q, m, p, :] = y[m // 2, :window_n]
     for copy in sent:
         copy.wait_send()
 
@@ -564,11 +582,12 @@
             pltpu.VMEM((pairs, sent, MAIN), BF),
             pltpu.VMEM((8, 128), F32),
             pltpu.VMEM((nz, 8, 128), F32),
-            pltpu.VMEM((2, 4, 128), F32),
-            pltpu.VMEM((ny, pairs, 4, 128), F32),
+            pltpu.VMEM((moms, 2, 128), F32),
+            pltpu.VMEM((ny, pairs, 2, 128), F32),
             dma((len(operands),)), dma((mates,)), dma((NX, moms)), dma((mates,)), dma((mates,)),
             dma((4, moms)), dma((mates,)), dma((pairs,)), dma((nz,)), dma((nz,)),
             dma((ny * mates,)), dma((ny, pairs)),
+            pltpu.SemaphoreType.REGULAR, pltpu.SemaphoreType.REGULAR,
         ],
         compiler_params=pltpu.CompilerParams(collective_id=0, has_side_effects=True),
     )(*operands)

time: 33.3 us -> 32.1 us (0.964)
  Pallas kernels: 32.5 us -> 31.3 us
    pallas_call x1, Pallas kernels: 31.8 us -> 30.6 us  [body(): pl.pallas_call(functools.partial(kernel, dims), out_shape=(pltpu.VMEM((ow...]
where the time goes in v3:
time: 32.1 us; the launch traced here: 32 us
  Pallas kernels  31.3 us (98%)
  between operations  0.64 us (2%)
    pallas_call x1, Pallas kernels, body(): pl.pallas_call(functools.partial(kernel, dims), out_shape=(pltpu.VMEM((ow...  30.6 us
    pallas_call x1, Pallas kernels, body(): pl.pallas_call(deliver, out_shape=tuple((jax.ShapeDtypeStruct(x.shape, x....  0.74 us

profile of v3, /device:TPU:1, one launch (start us, length us, event | category | flops | bytes accessed | tf_op | source)
XLA Modules:
  0.0 32.0 jit_solution(6421755960155250020)
XLA Ops:
  0.6 30.6 %shard_map.86 = (bf16[2,24,8,288]{3,2,1,0:T(8,128)(2,1)S(1)}, f32[2,3,8,24]{3,2,1,0:T(8,128)S(1)}) custom-call(bf16[2,24,8,288]{3,2,1,0:T(8,128)(2,1)} %gl_hbm.1, bf16[2,24,8,288]{3,2,1,0:T(8,128)(2,1)} %gg_hbm.1, f32[3,2,144]{2,1,0:T(2,128)} %bitcast.4, s32[2,4]{1,0:T(2,128)} %nb_hbm.1, bf16[2,8,3,8,24]{4,3,2,1,0:T(8,128)(2,1)} %bitcast.3, ...), custom_call_target="tpu_custom_call" | custom-call | tf_op jit(solution)/shard_map/pallas_call | solution.py:554
  31.3 0.7 %shard_map.87 = (bf16[2,24,8,288]{3,2,1,0:T(8,128)(2,1)}, f32[2,3,8,24]{3,2,1,0:T(8,128)}) custom-call(bf16[2,24,8,288]{3,2,1,0:T(8,128)(2,1)S(1)} %get-tuple-element.6.se_ref, f32[2,3,8,24]{3,2,1,0:T(8,128)S(1)} %get-tuple-element.7.pol_ref), custom_call_target="tpu_custom_call" | custom-call | tf_op jit(solution)/shard_map/pallas_call | solution.py:596

commit v4 on v3

--- a/solution.py
+++ b/solution.py
@@ -442,6 +442,25 @@
 
     window(1, 2)
     window_tail(2)
+    for rel in range(1, nz):
+        at = lax.rem(iz + rel, nz)
+        landed(got_z.at[at], r_z.at[at])
+    total = got_z[0]
+    for z in range(1, nz):
+        total = total + got_z[z]
+    swung = pltpu.roll(total, 64, 1)
+    for a in range(moms):
+        at = 3 * (a // 2)
+        low, high = (total, swung) if a % 2 == 0 else (swung, total)
+        plane[a, 0:1] = jnp.where(lane8[:1] < 64, low[at : at + 1], high[at + 1 : at + 2])
+        plane[a, 1:2] = low[at + 2 : at + 3]
+    got_p[iy, pair] = plane[me]
+    for i, (ry, rx, rm) in enumerate(flats):
+        send(remote(
+            plane.at[mom_of[rm]], got_p.at[iy, pair], s_p.at[i], r_p.at[iy, pair],
+            mom_of[rm], (y_of[ry] * nz + iz) * NX + ix_of[rx],
+        ))
+
     for a in range(moms):
         landed(gl_r.at[0, a], r_gl.at[0, a])
     spread_rows(0, has_low)
@@ -469,25 +488,6 @@
                 mom_of[rm], ring * NX + ix_of[rx],
             ))
     se_r[pair] = se_t[ix, me]
-
-    for rel in range(1, nz):
-        at = lax.rem(iz + rel, nz)
-        landed(got_z.at[at], r_z.at[at])
-    total = got_z[0]
-    for z in range(1, nz):
-        total = total + got_z[z]
-    swung = pltpu.roll(total, 64, 1)
-    for a in range(moms):
-        at = 3 * (a // 2)
-        low, high = (total, swung) if a % 2 == 0 else (swung, total)
-        plane[a, 0:1] = jnp.where(lane8[:1] < 64, low[at : at + 1], high[at + 1 : at + 2])
-        plane[a, 1:2] = low[at + 2 : at + 3]
-    got_p[iy, pair] = plane[me]
-    for i, (ry, rx, rm) in enumerate(flats):
-        send(remote(
-            plane.at[mom_of[rm]], got_p.at[iy, pair], s_p.at[i], r_p.at[iy, pair],
-            mom_of[rm], (y_of[ry] * nz + iz) * NX + ix_of[rx],
-        ))
 
     for i, (rx, rm) in enumerate(mates):
         if i:

time: 32.1 us -> 32.9 us (1.025)
  Pallas kernels: 31.3 us -> 32.2 us
    pallas_call x1, Pallas kernels: 30.6 us -> 31.5 us  [body(): pl.pallas_call(functools.partial(kernel, dims), out_shape=(pltpu.VMEM((ow...]
where the time goes in v4:
time: 32.9 us; the launch traced here: 32.8 us
  Pallas kernels  32.2 us (98%)
  between operations  0.64 us (2%)
    pallas_call x1, Pallas kernels, body(): pl.pallas_call(functools.partial(kernel, dims), out_shape=(pltpu.VMEM((ow...  31.5 us
    pallas_call x1, Pallas kernels, body(): pl.pallas_call(deliver, out_shape=tuple((jax.ShapeDtypeStruct(x.shape, x....  0.74 us

profile of v4, /device:TPU:1, one launch (start us, length us, event | category | flops | bytes accessed | tf_op | source)
XLA Modules:
  0.0 32.8 jit_solution(13044096785448024275)
XLA Ops:
  0.6 31.5 %shard_map.86 = (bf16[2,24,8,288]{3,2,1,0:T(8,128)(2,1)S(1)}, f32[2,3,8,24]{3,2,1,0:T(8,128)S(1)}) custom-call(bf16[2,24,8,288]{3,2,1,0:T(8,128)(2,1)} %gl_hbm.1, bf16[2,24,8,288]{3,2,1,0:T(8,128)(2,1)} %gg_hbm.1, f32[3,2,144]{2,1,0:T(2,128)} %bitcast.4, s32[2,4]{1,0:T(2,128)} %nb_hbm.1, bf16[2,8,3,8,24]{4,3,2,1,0:T(8,128)(2,1)} %bitcast.3, ...), custom_call_target="tpu_custom_call" | custom-call | tf_op jit(solution)/shard_map/pallas_call | solution.py:554
  32.1 0.7 %shard_map.87 = (bf16[2,24,8,288]{3,2,1,0:T(8,128)(2,1)}, f32[2,3,8,24]{3,2,1,0:T(8,128)}) custom-call(bf16[2,24,8,288]{3,2,1,0:T(8,128)(2,1)S(1)} %get-tuple-element.6.se_ref, f32[2,3,8,24]{3,2,1,0:T(8,128)S(1)} %get-tuple-element.7.pol_ref), custom_call_target="tpu_custom_call" | custom-call | tf_op jit(solution)/shard_map/pallas_call | solution.py:596
